TPU v7x, 32 devices: a whole 2x2x4 slice. The times are simulated.
32 devices in a mesh: league: 4 (over x, core), env: 8 (over z, y).
Axes of the slice: x: 2, y: 2, z: 4, core: 2. Of those that a mesh axis runs over, the one named last changes fastest.
Arguments:
- obs_own: bfloat16 [4, 2, 128, 16, 2048], P('league', None, 'env'), may hold values from -6 to 6
- obs_opp: bfloat16 [4, 2, 128, 16, 2048], P('league', None, 'env'), may hold values from -6 to 6
- actions: int32 [4, 2, 2, 128, 16], P('league', None, None, 'env'), may hold values from 0 to 255
- opponent_picks: int32 [4, 2], P('league'), may hold values from 0 to 3
- policy_weight: bfloat16 [4, 2048, 2048], P('league', 'env'), may hold values from -0.125 to 0.125
- policy_gain: bfloat16 [4, 2048], P('league'), may hold values from 0.25 to 1.75
- action_table: bfloat16 [256, 2048], replicated, may hold values from -6 to 6
- value_gain: bfloat16 [2048], replicated, may hold values from 0.25 to 1.75
- value_up: bfloat16 [2048, 1024], replicated, may hold values from -0.125 to 0.125
- value_out: bfloat16 [1024], replicated, may hold values from -0.1875 to 0.1875
Outputs:
- learner_rows: bfloat16 [4, 2, 16, 2048, 128], P('league', None, None, 'env')
- values: float32 [4, 2, 128, 16], P('league', None, 'env')
All inputs are finite; a program needn't handle non-finite values.
Results may differ from a plain program's by a relative error of at most 0.0054.
Values may be sent and summed in bfloat16 or wider, within the bound.
A program may use at most 128 MiB of HBM per device.

v0:
```python
import jax
import jax.numpy as jnp
from jax import lax
from jax.sharding import PartitionSpec as P


def rms_norm(inputs, gain):
    scale = lax.rsqrt(jnp.mean(inputs * inputs, axis=-1, keepdims=True) + 1e-05)
    return inputs * scale * gain.astype(jnp.float32)


def local(
    obs_own,
    obs_opp,
    actions,
    opponent_picks,
    policy_weight,
    policy_gain,
    action_table,
    value_gain,
    value_up,
    value_out,
):
    round_count = obs_own.shape[1]
    env_count = obs_own.shape[2]
    step_count = obs_own.shape[3]
    model_width = obs_own.shape[4]
    row_count = env_count * step_count
    weight_shard = policy_weight[0]
    own_gain = policy_gain[0]
    group_count = lax.axis_size("league")
    my_group = lax.axis_index("league")
    own_inputs = obs_own[0].reshape(round_count * row_count, model_width).astype(jnp.float32)
    own_normed = rms_norm(own_inputs, own_gain).astype(jnp.bfloat16)
    own_whole = lax.all_gather(weight_shard, "env", axis=0, tiled=True)
    own_state = own_inputs + jnp.dot(own_normed, own_whole, preferred_element_type=jnp.float32)
    every_pick = lax.all_gather(opponent_picks, "league", axis=0, tiled=True)
    action_range = jnp.arange(action_table.shape[0], dtype=jnp.int32)
    traj_list = []
    value_list = []
    for round_index in range(round_count):
        opp_raw = obs_opp[0, round_index].reshape(row_count, model_width)
        opp_inputs = opp_raw.astype(jnp.float32)
        all_rows = lax.all_gather(opp_raw, "league", axis=0, tiled=True)
        all_normed = rms_norm(all_rows.astype(jnp.float32), own_gain).astype(jnp.bfloat16)
        products = jnp.dot(all_normed, own_whole, preferred_element_type=jnp.float32)
        served = (every_pick[:, round_index] == my_group).astype(jnp.float32)
        products = (
            products.reshape(group_count, row_count, model_width) * served[:, None, None]
        ).astype(jnp.bfloat16)
        answers = lax.all_to_all(products, "league", split_axis=0, concat_axis=0, tiled=True)
        opp_state = opp_inputs + jnp.sum(answers.astype(jnp.float32), axis=0)
        own_ids = actions[0, 0, round_index].reshape(row_count)
        opp_ids = actions[0, 1, round_index].reshape(row_count)
        onehot = (own_ids[:, None] == action_range[None, :]).astype(jnp.bfloat16) + (
            opp_ids[:, None] == action_range[None, :]
        ).astype(jnp.bfloat16)
        action_sum = jnp.dot(onehot, action_table, preferred_element_type=jnp.float32)
        round_state = lax.dynamic_slice_in_dim(own_state, round_index * row_count, row_count, 0)
        joint_sum = round_state + opp_state + action_sum
        joint_row = rms_norm(joint_sum, value_gain).astype(jnp.bfloat16)
        value_hidden = jax.nn.silu(
            jnp.dot(joint_row, value_up, preferred_element_type=jnp.float32)
        ).astype(jnp.bfloat16)
        value_est = jnp.dot(value_hidden, value_out, preferred_element_type=jnp.float32)
        value_list.append(value_est.reshape(env_count, step_count))
        time_block = joint_row.reshape(env_count, step_count, model_width).transpose(1, 2, 0)
        traj_list.append(lax.all_to_all(time_block, "env", split_axis=1, concat_axis=2, tiled=True))
    learner_rows = jnp.stack(traj_list)
    values = jnp.stack(value_list)
    return (learner_rows[None], values[None])


def solution(mesh):
    in_specs = (
        P("league", None, "env", None, None),
        P("league", None, "env", None, None),
        P("league", None, None, "env", None),
        P("league", None),
        P("league", "env", None),
        P("league", None),
        P(),
        P(),
        P(),
        P(),
    )
    out_specs = (P("league", None, None, "env", None), P("league", None, "env", None))
    return jax.shard_map(local, mesh=mesh, in_specs=in_specs, out_specs=out_specs, check_vma=False)
```

profile of v0, /device:TPU:0, one launch (start us, length us, event | category | flops | bytes accessed | tf_op | source)
XLA Modules:
  0.0 430.5 jit_solution(11888221236370943280)
XLA Ops:
  12.0 6.0 %all-gather.1 = s32[4,1,2]{2,1,0:T(1,128)S(1)} all-gather(s32[1,1,2]{2,1,0:T(1,128)S(1)} %bitcast.90), channel_id=1, replica_groups=mesh['league'=4,'env'=8] {'league'}, dimensions={0}, use_global_device_ids=true | all-gather | bytes 40 | tf_op jit(solution)/shard_map/all_gather | solution.py:37
  18.0 29.8 %all-gather.6.cloned.1.call-done = bf16[1024,2048]{1,0:T(8,128)(2,1)} async-done(((bf16[256,2048]{1,0:T(8,128)(2,1)}), bf16[1024,2048]{1,0:T(8,128)(2,1)}) %all-gather.6.cloned.1.call-update) | async-done | bytes 4194320 | tf_op jit(solution)/shard_map/all_gather | solution.py:44
  50.9 124.0 %all-gather.10.cloned.1.call-done = bf16[1,2048,2048]{2,1,0:T(8,128)(2,1)} async-done(((bf16[1,256,2048]{2,1,0:T(8,128)(2,1)}), bf16[1,2048,2048]{2,1,0:T(8,128)(2,1)}) %all-gather.10.cloned.1.call-update) | async-done | bytes 8388624 | tf_op jit(solution)/shard_map/all_gather | solution.py:35
  174.9 12.6 %fusion.8 = f32[1024,2048]{1,0:T(8,128)S(1)} fusion(bf16[1,2048,2048]{2,1,0:T(8,128)(2,1)} %all-gather.10.cloned.1.call-done, bf16[1024,2048]{1,0:T(8,128)(2,1)} %all-gather.6.cloned.1.call-done, f32[2048]{0:T(1024)S(1)} %bitcast.84, f32[1024]{0:T(1024)S(1)} %add_rsqrt_fusion.2), kind=kOutput, calls=%fused_computation.12 | convolution fusion | flops 8598323200 | bytes 20983808 | tf_op jit(solution)/shard_map/dot_general | solution.py:46
  190.7 4.9 %all-to-all-start = ((bf16[4,256,2048]{2,1,0:T(8,128)(2,1)}), bf16[4,256,2048]{2,1,0:T(8,128)(2,1)}, u32[]{:S(2)}, u32[]{:S(2)}) async-start(bf16[4,256,2048]{2,1,0:T(8,128)(2,1)} %multiply_convert_fusion.1), calls=%async_computation | async-start | bytes 8388608 | tf_op jit(solution)/shard_map/all_to_all | solution.py:51
  195.6 22.4 %all-gather.8.cloned.1.call-done = bf16[1024,2048]{1,0:T(8,128)(2,1)} async-done(((bf16[256,2048]{1,0:T(8,128)(2,1)}), bf16[1024,2048]{1,0:T(8,128)(2,1)}) %all-gather.8.cloned.1.call-update) | async-done | bytes 4194320 | tf_op jit(solution)/shard_map/all_gather | solution.py:44
  221.4 11.3 %fusion.6 = f32[1024,2048]{1,0:T(8,128)S(1)} fusion(bf16[1,2048,2048]{2,1,0:T(8,128)(2,1)} %all-gather.10.cloned.1.call-done, bf16[1024,2048]{1,0:T(8,128)(2,1)S(1)} %copy-done.7, f32[1024]{0:T(1024)S(1)} %add_rsqrt_fusion.1, f32[2048]{0:T(1024)S(1)} %bitcast.85), kind=kOutput, calls=%fused_computation.10 | convolution fusion | flops 8598323200 | bytes 20983808 | tf_op jit(solution)/shard_map/dot_general | solution.py:46
  235.9 16.6 %all-to-all-done = bf16[4,256,2048]{2,1,0:T(8,128)(2,1)} async-done(((bf16[4,256,2048]{2,1,0:T(8,128)(2,1)}), bf16[4,256,2048]{2,1,0:T(8,128)(2,1)}, u32[]{:S(2)}, u32[]{:S(2)}) %all-to-all-start) | async-done | bytes 4194336 | tf_op jit(solution)/shard_map/all_to_all | solution.py:51
  252.6 5.0 %all-to-all-start.2 = ((bf16[4,256,2048]{2,1,0:T(8,128)(2,1)}), bf16[4,256,2048]{2,1,0:T(8,128)(2,1)}, u32[]{:S(2)}, u32[]{:S(2)}) async-start(bf16[4,256,2048]{2,1,0:T(8,128)(2,1)} %multiply_convert_fusion), calls=%async_computation.2 | async-start | bytes 8388608 | tf_op jit(solution)/shard_map/all_to_all | solution.py:51
  259.1 7.0 %bitcast_add_fusion = f32[512,2048]{1,0:T(8,128)S(1)} fusion(bf16[1,2,16,16,2048]{4,3,2,1,0:T(8,128)(2,1)S(1)} %copy-done.4, bf16[512,2048]{1,0:T(8,128)(2,1)S(1)} %fusion.16, bf16[1,2048,2048]{2,1,0:T(8,128)(2,1)} %all-gather.10.cloned.1.call-done), kind=kOutput, calls=%fused_computation.20 | convolution fusion | flops 4297064448 | bytes 16777216 | tf_op jit(solution)/shard_map/dot_general | solution.py:36
  266.1 4.8 %convert_reduce_fusion.1 = f32[256,2048]{1,0:T(8,128)S(1)} fusion(bf16[4,256,2048]{2,1,0:T(8,128)(2,1)} %all-to-all-done), kind=kLoop, calls=%fused_computation.18 | loop fusion | flops 3670016 | bytes 6291456 | tf_op jit(solution)/shard_map/reduce_sum | solution.py:52
  273.1 32.6 %all-to-all-done.2 = bf16[4,256,2048]{2,1,0:T(8,128)(2,1)} async-done(((bf16[4,256,2048]{2,1,0:T(8,128)(2,1)}), bf16[4,256,2048]{2,1,0:T(8,128)(2,1)}, u32[]{:S(2)}, u32[]{:S(2)}) %all-to-all-start.2) | async-done | bytes 4194336 | tf_op jit(solution)/shard_map/all_to_all | solution.py:51
  311.2 8.8 %copy.27 = bf16[16,16,2048]{0,1,2:T(8,128)(2,1)} copy(bf16[16,16,2048]{2,1,0:T(8,128)(2,1)S(1)} %bitcast.81) | data formatting | bytes 2097152 | tf_op jit(solution)/shard_map/reshape | solution.py:67
  320.0 7.5 %bitcast_bitcast_fusion = bf16[2048,16,16]{2,1,0:T(8,128)(2,1)} fusion(bf16[16,16,2048]{0,1,2:T(8,128)(2,1)} %copy.27), kind=kLoop, calls=%fused_computation.71 | loop fusion | bytes 2097152
  327.5 11.2 %reshape.109 = bf16[8,2,32768]{2,1,0:T(2,128)(2,1)} reshape(bf16[2048,16,16]{2,1,0:T(8,128)(2,1)} %bitcast_bitcast_fusion) | data formatting | bytes 2097152
  338.7 5.5 %all-to-all-start.3 = ((bf16[8,2,32768]{2,1,0:T(2,128)(2,1)}), bf16[8,2,32768]{2,1,0:T(2,128)(2,1)S(1)}, u32[]{:S(2)}, u32[]{:S(2)}) async-start(bf16[8,2,32768]{2,1,0:T(2,128)(2,1)} %reshape.109), calls=%async_computation.3 | async-start | bytes 2097152 | tf_op jit(solution)/shard_map/all_to_all | solution.py:68
  344.2 8.8 %copy.24 = bf16[16,16,2048]{0,1,2:T(8,128)(2,1)} copy(bf16[16,16,2048]{2,1,0:T(8,128)(2,1)S(1)} %bitcast.80) | data formatting | bytes 2097152 | tf_op jit(solution)/shard_map/reshape | solution.py:67
  353.1 7.5 %bitcast_bitcast_fusion.1 = bf16[2048,16,16]{2,1,0:T(8,128)(2,1)} fusion(bf16[16,16,2048]{0,1,2:T(8,128)(2,1)} %copy.24), kind=kLoop, calls=%fused_computation.72 | loop fusion | bytes 2097152
  360.5 11.2 %reshape.111 = bf16[8,2,32768]{2,1,0:T(2,128)(2,1)} reshape(bf16[2048,16,16]{2,1,0:T(8,128)(2,1)} %bitcast_bitcast_fusion.1) | data formatting | bytes 2097152
  371.8 6.0 %all-to-all-start.1 = ((bf16[8,2,32768]{2,1,0:T(2,128)(2,1)}), bf16[8,2,32768]{2,1,0:T(2,128)(2,1)S(1)}, u32[]{:S(2)}, u32[]{:S(2)}) async-start(bf16[8,2,32768]{2,1,0:T(2,128)(2,1)} %reshape.111), calls=%async_computation.1 | async-start | bytes 2097152 | tf_op jit(solution)/shard_map/all_to_all | solution.py:68
  386.5 7.6 %reshape.110 = bf16[2048,16,16]{2,1,0:T(8,128)(2,1)} reshape(bf16[8,2,32768]{2,1,0:T(2,128)(2,1)S(1)} %all-to-all-done.3) | data formatting | bytes 2097152
  394.1 9.1 %copy.29 = bf16[16,256,8,16]{1,3,2,0:T(8,128)(2,1)} copy(bf16[16,256,8,16]{3,0,1,2:T(8,128)(2,1)} %bitcast.72) | data formatting | bytes 2097152 | tf_op jit(solution)/shard_map/all_to_all | solution.py:68
  403.2 7.6 %reshape.112 = bf16[2048,16,16]{2,1,0:T(8,128)(2,1)} reshape(bf16[8,2,32768]{2,1,0:T(2,128)(2,1)S(1)} %all-to-all-done.1) | data formatting | bytes 2097152
  410.8 9.1 %copy.26 = bf16[16,256,8,16]{1,3,2,0:T(8,128)(2,1)} copy(bf16[16,256,8,16]{3,0,1,2:T(8,128)(2,1)} %bitcast.73) | data formatting | bytes 2097152 | tf_op jit(solution)/shard_map/all_to_all | solution.py:68
  (71 shorter events, 39.6 us)
Async XLA Ops:
  7.2 263.8 %copy-start = (bf16[256,2048]{1,0:T(8,128)(2,1)S(1)}, bf16[256,2048]{1,0:T(8,128)(2,1)}, u32[]{:S(2)}) copy-start(bf16[256,2048]{1,0:T(8,128)(2,1)} %param.16) | copy-start | bytes 3145732
  7.2 4.8 %copy-start.14 = (s32[1,2]{1,0:T(1,128)S(1)}, s32[1,2]{1,0:T(1,128)}, u32[]{:S(2)}) copy-start(s32[1,2]{1,0:T(1,128)} %param.13) | copy-start | bytes 28
  7.2 10.7 %copy-start.11 = (bf16[1,2048]{1,0:T(2,128)(2,1)S(1)}, bf16[1,2048]{1,0:T(2,128)(2,1)}, u32[]{:S(2)}) copy-start(bf16[1,2048]{1,0:T(2,128)(2,1)} %param.15) | copy-start | bytes 12292
  7.2 40.6 %all-gather.6.cloned.1.call-start = ((), (), s32[]{:S(2)}) async-start(), calls=%async_computation.4 | async-start | bytes 5242880 | tf_op jit(solution)/shard_map/all_gather | solution.py:44
  10.5 164.4 %all-gather.10.cloned.1.call-start = ((), (), s32[]{:S(2)}) async-start(), calls=%async_computation.6 | async-start | bytes 9437184 | tf_op jit(solution)/shard_map/all_gather | solution.py:35
  11.2 206.8 %all-gather.8.cloned.1.call-start = ((), (), s32[]{:S(2)}) async-start(), calls=%async_computation.5 | async-start | bytes 5242880 | tf_op jit(solution)/shard_map/all_gather | solution.py:44
  190.7 61.9 %all-to-all-start = ((bf16[4,256,2048]{2,1,0:T(8,128)(2,1)}), bf16[4,256,2048]{2,1,0:T(8,128)(2,1)}, u32[]{:S(2)}, u32[]{:S(2)}) async-start(bf16[4,256,2048]{2,1,0:T(8,128)(2,1)} %multiply_convert_fusion.1), calls=%async_computation | async-start | bytes 8388608 | tf_op jit(solution)/shard_map/all_to_all | solution.py:51
  218.0 3.4 copy-start.7
  235.9 21.7 %copy-start.10 = (s32[1,2,2,16,16]{4,3,2,1,0:T(8,128)S(1)}, s32[1,2,2,16,16]{4,3,2,1,0:T(8,128)}, u32[]{:S(2)}) copy-start(s32[1,2,2,16,16]{4,3,2,1,0:T(8,128)} %param.12) | copy-start | bytes 12292
  235.9 21.9 %copy-start.4 = (bf16[1,2,16,16,2048]{4,3,2,1,0:T(8,128)(2,1)S(1)}, bf16[1,2,16,16,2048]{4,3,2,1,0:T(8,128)(2,1)}, u32[]{:S(2)}) copy-start(bf16[1,2,16,16,2048]{4,3,2,1,0:T(8,128)(2,1)} %param.10) | copy-start | bytes 6291460
  235.9 22.4 %copy-start.12 = (bf16[2048]{0:T(1024)(128)(2,1)S(1)}, bf16[2048]{0:T(1024)(128)(2,1)}, u32[]{:S(2)}) copy-start(bf16[2048]{0:T(1024)(128)(2,1)} %param.17) | copy-start | bytes 12292
  252.6 53.1 %all-to-all-start.2 = ((bf16[4,256,2048]{2,1,0:T(8,128)(2,1)}), bf16[4,256,2048]{2,1,0:T(8,128)(2,1)}, u32[]{:S(2)}, u32[]{:S(2)}) async-start(bf16[4,256,2048]{2,1,0:T(8,128)(2,1)} %multiply_convert_fusion), calls=%async_computation.2 | async-start | bytes 8388608 | tf_op jit(solution)/shard_map/all_to_all | solution.py:51
  266.1 4.9 %copy-start.5 = (f32[512,2048]{1,0:T(8,128)}, f32[512,2048]{1,0:T(8,128)S(1)}, u32[]{:S(2)}) copy-start(f32[512,2048]{1,0:T(8,128)S(1)} %bitcast_add_fusion) | copy-start | bytes 12582916
  266.1 4.9 %copy-start.2 = (bf16[1,1,16,16,2048]{4,3,2,1,0:T(8,128)(2,1)S(1)}, bf16[1,1,16,16,2048]{4,3,2,1,0:T(8,128)(2,1)}, u32[]{:S(2)}) copy-start(bf16[1,1,16,16,2048]{4,3,2,1,0:T(8,128)(2,1)} %get-tuple-element.8) | copy-start | bytes 3145732
  273.1 36.0 %copy-start.1 = (bf16[1,1,16,16,2048]{4,3,2,1,0:T(8,128)(2,1)S(1)}, bf16[1,1,16,16,2048]{4,3,2,1,0:T(8,128)(2,1)}, u32[]{:S(2)}) copy-start(bf16[1,1,16,16,2048]{4,3,2,1,0:T(8,128)(2,1)} %get-tuple-element.9) | copy-start | bytes 3145732
  305.7 3.4 copy-start.6
  309.1 1.6 copy-start.3
  311.1 8.8 %copy-start.9 = (bf16[256,2048]{1,0:T(8,128)(2,1)}, bf16[256,2048]{1,0:T(8,128)(2,1)S(1)}, u32[]{:S(2)}) copy-start(bf16[256,2048]{1,0:T(8,128)(2,1)S(1)} %get-tuple-element.15) | copy-start | bytes 3145732
  311.2 33.1 %copy-start.8 = (bf16[256,2048]{1,0:T(8,128)(2,1)}, bf16[256,2048]{1,0:T(8,128)(2,1)S(1)}, u32[]{:S(2)}) copy-start(bf16[256,2048]{1,0:T(8,128)(2,1)S(1)} %get-tuple-element.14) | copy-start | bytes 3145732
  338.7 33.1 %all-to-all-start.3 = ((bf16[8,2,32768]{2,1,0:T(2,128)(2,1)}), bf16[8,2,32768]{2,1,0:T(2,128)(2,1)S(1)}, u32[]{:S(2)}, u32[]{:S(2)}) async-start(bf16[8,2,32768]{2,1,0:T(2,128)(2,1)} %reshape.109), calls=%async_computation.3 | async-start | bytes 2097152 | tf_op jit(solution)/shard_map/all_to_all | solution.py:68
  360.5 17.2 %copy-start.13 = (bf16[1024]{0:T(1024)(128)(2,1)S(1)}, bf16[1024]{0:T(1024)(128)(2,1)}, u32[]{:S(2)}) copy-start(bf16[1024]{0:T(1024)(128)(2,1)} %param.19) | copy-start | bytes 6148
  371.8 31.4 %all-to-all-start.1 = ((bf16[8,2,32768]{2,1,0:T(2,128)(2,1)}), bf16[8,2,32768]{2,1,0:T(2,128)(2,1)S(1)}, u32[]{:S(2)}, u32[]{:S(2)}) async-start(bf16[8,2,32768]{2,1,0:T(2,128)(2,1)} %reshape.111), calls=%async_computation.1 | async-start | bytes 2097152 | tf_op jit(solution)/shard_map/all_to_all | solution.py:68
Sparse Core Ops, SparseCore 0:
  10.6 37.1 all-gather.5
  49.9 124.9 all-gather.9
  176.5 41.4 all-gather.7
where the time goes:
time: 432 us; the launch traced here: 431 us
  waiting for transfers between devices  227 us (53%)
  local copies, waits for them, and re-layouts  95.7 us (22%)
  matrix products  41.7 us (10%)
  other arithmetic  24.9 us (6%)
  starting transfers between devices  21.6 us (5%)
  between operations  14 us (3%)
  blocking collectives  5.95 us (1%)
    all_gather x1, waiting for transfers between devices, local(): own_whole = lax.all_gather(weight_shard, 'env', axis=0, tiled=True)  124 us
    unnamed x38, local copies, waits for them, and re-layouts  56 us
    all_gather x2, waiting for transfers between devices, local(): all_rows = lax.all_gather(opp_raw, 'league', axis=0, tiled=True)  52.1 us
    all_to_all x2, waiting for transfers between devices, local(): lax.all_to_all(products, 'league', split_axis=0, concat_axis=0, tiled=True)  49.2 us
    dot_general x2, matrix products, local(): jnp.dot(all_normed, own_whole, preferred_element_type=jnp.float32)  23.9 us
    all_to_all x2, local copies, waits for them, and re-layouts, local(): lax.all_to_all(time_block, 'env', split_axis=1, concat_axis=2, tiled=True)  18.2 us
    reshape x2, local copies, waits for them, and re-layouts, local(): joint_row.reshape(env_count, step_count, model_width).transpose(1, 2, 0)  17.7 us
    all_to_all x2, starting transfers between devices, local(): lax.all_to_all(time_block, 'env', split_axis=1, concat_axis=2, tiled=True)  11.5 us
  transfers between devices with their start and end apart: 7, of which 5 were waited for; matrix products, arithmetic and copies ran while one was open for 24% of the time, Pallas kernels for 0%

commit v1 on v0

--- a/solution.py
+++ b/solution.py
@@ -2,6 +2,27 @@
 import jax.numpy as jnp
 from jax import lax
 from jax.sharding import PartitionSpec as P
+
+
+def gather_around(x, axis, dim):
+    size, mine, width = (lax.axis_size(axis), lax.axis_index(axis), x.shape[dim])
+    right = [(i, (i + 1) % size) for i in range(size)]
+    left = [(i, (i - 1) % size) for i in range(size)]
+    filled = jnp.zeros((*x.shape[:dim], size * width, *x.shape[dim + 1 :]), x.dtype)
+    filled = lax.dynamic_update_slice_in_dim(filled, x, mine * width, axis=dim)
+    from_left = from_right = x
+    half = size // 2
+    for step in range(1, half + 1):
+        from_left = lax.ppermute(from_left, axis, right)
+        filled = lax.dynamic_update_slice_in_dim(
+            filled, from_left, (mine - step) % size * width, axis=dim
+        )
+        if step < size - half:
+            from_right = lax.ppermute(from_right, axis, left)
+            filled = lax.dynamic_update_slice_in_dim(
+                filled, from_right, (mine + step) % size * width, axis=dim
+            )
+    return filled
 
 
 def rms_norm(inputs, gain):
@@ -41,7 +62,7 @@
     for round_index in range(round_count):
         opp_raw = obs_opp[0, round_index].reshape(row_count, model_width)
         opp_inputs = opp_raw.astype(jnp.float32)
-        all_rows = lax.all_gather(opp_raw, "league", axis=0, tiled=True)
+        all_rows = gather_around(opp_raw, "league", 0)
         all_normed = rms_norm(all_rows.astype(jnp.float32), own_gain).astype(jnp.bfloat16)
         products = jnp.dot(all_normed, own_whole, preferred_element_type=jnp.float32)
         served = (every_pick[:, round_index] == my_group).astype(jnp.float32)

time: 432 us -> 385 us (0.89)
  waiting for transfers between devices: 227 us -> 123 us
  blocking collectives: 5.95 us -> 41.4 us
  local copies, waits for them, and re-layouts: 95.7 us -> 111 us
    all_gather x1, waiting for transfers between devices: 124 us -> 46.3 us  [local(): own_whole = lax.all_gather(weight_shard, 'env', axis=0, tiled=True)]
    all_gather x2 -> x0, waiting for transfers between devices: 52.1 us -> none  [local(): all_rows = lax.all_gather(opp_raw, 'league', axis=0, tiled=True)]
    all_gather x1, blocking collectives: 5.95 us -> 41.4 us  [local(): every_pick = lax.all_gather(opponent_picks, 'league', axis=0, tiled=True)]
    ppermute x0 -> x6, waiting for transfers between devices: none -> 14.2 us  [the longest x4 14.2 us: gather_around(): from_left = lax.ppermute(from_left, axis, right)]
    dynamic_update_slice x0 -> x7, local copies, waits for them, and re-layouts: none -> 13.9 us  [the longest x3 8.06 us: gather_around(): lax.dynamic_update_slice_in_dim(filled, from_left, (mine - step) % size *...]
    all_to_all x2, waiting for transfers between devices: 49.2 us -> 61.6 us  [local(): lax.all_to_all(products, 'league', split_axis=0, concat_axis=0, tiled=True)]
    ppermute x0 -> x6, starting transfers between devices: none -> 5.65 us  [the longest x4 5.52 us: gather_around(): from_left = lax.ppermute(from_left, axis, right)]
  transfers between devices with their start and end apart: 7 -> 11, of which waited for: 5 -> 6; matrix products, arithmetic and copies ran while one was open for 24% -> 29% of each run, Pallas kernels for 0% -> 0%
where the time goes in v1:
time: 385 us; the launch traced here: 383 us
  waiting for transfers between devices  123 us (32%)
  local copies, waits for them, and re-layouts  111 us (29%)
  matrix products  41.7 us (11%)
  blocking collectives  41.4 us (11%)
  other arithmetic  26.4 us (7%)
  starting transfers between devices  25.3 us (7%)
  between operations  14.3 us (4%)
    all_to_all x2, waiting for transfers between devices, local(): lax.all_to_all(products, 'league', split_axis=0, concat_axis=0, tiled=True)  61.6 us
    unnamed x38, local copies, waits for them, and re-layouts  56 us
    all_gather x1, waiting for transfers between devices, local(): own_whole = lax.all_gather(weight_shard, 'env', axis=0, tiled=True)  46.3 us
    all_gather x1, blocking collectives, local(): every_pick = lax.all_gather(opponent_picks, 'league', axis=0, tiled=True)  41.4 us
    dot_general x2, matrix products, local(): jnp.dot(all_normed, own_whole, preferred_element_type=jnp.float32)  23.9 us
    all_to_all x2, local copies, waits for them, and re-layouts, local(): lax.all_to_all(time_block, 'env', split_axis=1, concat_axis=2, tiled=True)  18.2 us
    reshape x2, local copies, waits for them, and re-layouts, local(): joint_row.reshape(env_count, step_count, model_width).transpose(1, 2, 0)  17.7 us
    ppermute x4, waiting for transfers between devices, gather_around(): from_left = lax.ppermute(from_left, axis, right)  14.2 us
  transfers between devices with their start and end apart: 11, of which 6 were waited for; matrix products, arithmetic and copies ran while one was open for 29% of the time, Pallas kernels for 0%

profile of v1, /device:TPU:0, one launch (start us, length us, event | category | flops | bytes accessed | tf_op | source)
XLA Modules:
  0.0 383.1 jit_solution(6959375198091400153)
XLA Ops:
  17.6 41.4 %all-gather.1 = s32[4,1,2]{2,1,0:T(1,128)S(1)} all-gather(s32[1,1,2]{2,1,0:T(1,128)S(1)} %bitcast.94), channel_id=1, replica_groups=mesh['league'=4,'env'=8] {'league'}, dimensions={0}, use_global_device_ids=true | all-gather | bytes 40 | tf_op jit(solution)/shard_map/all_gather | solution.py:58
  74.1 11.2 %collective-permute-done.5 = bf16[256,2048]{1,0:T(8,128)(2,1)} collective-permute-done((bf16[256,2048]{1,0:T(8,128)(2,1)}, bf16[256,2048]{1,0:T(8,128)(2,1)}, u32[]{:S(2)}, u32[]{:S(2)}) %collective-permute-start.5) | collective-permute-done | bytes 1048608 | tf_op jit(solution)/shard_map/ppermute | solution.py:16
  91.6 46.3 %all-gather.4.cloned.1.call-done = bf16[1,2048,2048]{2,1,0:T(8,128)(2,1)} async-done(((bf16[1,256,2048]{2,1,0:T(8,128)(2,1)}), bf16[1,2048,2048]{2,1,0:T(8,128)(2,1)}) %all-gather.4.cloned.1.call-update) | async-done | bytes 8388624 | tf_op jit(solution)/shard_map/all_gather | solution.py:56
  137.8 12.6 %fusion.6 = f32[1024,2048]{1,0:T(8,128)S(1)} fusion(bf16[1,2048,2048]{2,1,0:T(8,128)(2,1)} %all-gather.4.cloned.1.call-done, bf16[1024,2048]{1,0:T(8,128)(2,1)} %get-tuple-element.22, f32[1024]{0:T(1024)S(1)} %add_rsqrt_fusion.1, f32[2048]{0:T(1024)S(1)} %bitcast.88), kind=kOutput, calls=%fused_computation.10 | convolution fusion | flops 8598323200 | bytes 20983808 | tf_op jit(solution)/shard_map/dot_general | solution.py:67
  153.6 5.1 %all-to-all-start.2 = ((bf16[4,256,2048]{2,1,0:T(8,128)(2,1)}), bf16[4,256,2048]{2,1,0:T(8,128)(2,1)}, u32[]{:S(2)}, u32[]{:S(2)}) async-start(bf16[4,256,2048]{2,1,0:T(8,128)(2,1)} %multiply_convert_fusion), calls=%async_computation.2 | async-start | bytes 8388608 | tf_op jit(solution)/shard_map/all_to_all | solution.py:72
  162.2 11.3 %fusion.8 = f32[1024,2048]{1,0:T(8,128)S(1)} fusion(bf16[1,2048,2048]{2,1,0:T(8,128)(2,1)} %all-gather.4.cloned.1.call-done, bf16[1024,2048]{1,0:T(8,128)(2,1)S(1)} %copy-done.2, f32[2048]{0:T(1024)S(1)} %bitcast.89, f32[1024]{0:T(1024)S(1)} %add_rsqrt_fusion.2), kind=kOutput, calls=%fused_computation.12 | convolution fusion | flops 8598323200 | bytes 20983808 | tf_op jit(solution)/shard_map/dot_general | solution.py:67
  176.7 30.1 %all-to-all-done.2 = bf16[4,256,2048]{2,1,0:T(8,128)(2,1)} async-done(((bf16[4,256,2048]{2,1,0:T(8,128)(2,1)}), bf16[4,256,2048]{2,1,0:T(8,128)(2,1)}, u32[]{:S(2)}, u32[]{:S(2)}) %all-to-all-start.2) | async-done | bytes 4194336 | tf_op jit(solution)/shard_map/all_to_all | solution.py:72
  206.8 5.1 %all-to-all-start = ((bf16[4,256,2048]{2,1,0:T(8,128)(2,1)}), bf16[4,256,2048]{2,1,0:T(8,128)(2,1)}, u32[]{:S(2)}, u32[]{:S(2)}) async-start(bf16[4,256,2048]{2,1,0:T(8,128)(2,1)} %multiply_convert_fusion.1), calls=%async_computation | async-start | bytes 8388608 | tf_op jit(solution)/shard_map/all_to_all | solution.py:72
  214.6 7.0 %bitcast_add_fusion = f32[512,2048]{1,0:T(8,128)S(1)} fusion(bf16[1,2,16,16,2048]{4,3,2,1,0:T(8,128)(2,1)S(1)} %copy-done.5, bf16[512,2048]{1,0:T(8,128)(2,1)S(1)} %fusion.16, bf16[1,2048,2048]{2,1,0:T(8,128)(2,1)} %all-gather.4.cloned.1.call-done), kind=kOutput, calls=%fused_computation.20 | convolution fusion | flops 4297064448 | bytes 16777216 | tf_op jit(solution)/shard_map/dot_general | solution.py:57
  221.6 4.6 %convert_reduce_fusion = f32[256,2048]{1,0:T(8,128)S(1)} fusion(bf16[4,256,2048]{2,1,0:T(8,128)(2,1)} %all-to-all-done.2), kind=kLoop, calls=%fused_computation.16 | loop fusion | flops 3670016 | bytes 6291456 | tf_op jit(solution)/shard_map/reduce_sum | solution.py:73
  228.3 31.5 %all-to-all-done = bf16[4,256,2048]{2,1,0:T(8,128)(2,1)} async-done(((bf16[4,256,2048]{2,1,0:T(8,128)(2,1)}), bf16[4,256,2048]{2,1,0:T(8,128)(2,1)}, u32[]{:S(2)}, u32[]{:S(2)}) %all-to-all-start) | async-done | bytes 4194336 | tf_op jit(solution)/shard_map/all_to_all | solution.py:72
  265.3 8.8 %copy.24 = bf16[16,16,2048]{0,1,2:T(8,128)(2,1)} copy(bf16[16,16,2048]{2,1,0:T(8,128)(2,1)S(1)} %bitcast.85) | data formatting | bytes 2097152 | tf_op jit(solution)/shard_map/reshape | solution.py:88
  274.2 7.5 %bitcast_bitcast_fusion.1 = bf16[2048,16,16]{2,1,0:T(8,128)(2,1)} fusion(bf16[16,16,2048]{0,1,2:T(8,128)(2,1)} %copy.24), kind=kLoop, calls=%fused_computation.80 | loop fusion | bytes 2097152
  281.6 11.2 %reshape.111 = bf16[8,2,32768]{2,1,0:T(2,128)(2,1)} reshape(bf16[2048,16,16]{2,1,0:T(8,128)(2,1)} %bitcast_bitcast_fusion.1) | data formatting | bytes 2097152
  296.5 8.8 %copy.27 = bf16[16,16,2048]{0,1,2:T(8,128)(2,1)} copy(bf16[16,16,2048]{2,1,0:T(8,128)(2,1)S(1)} %bitcast.84) | data formatting | bytes 2097152 | tf_op jit(solution)/shard_map/reshape | solution.py:88
  305.3 7.5 %bitcast_bitcast_fusion = bf16[2048,16,16]{2,1,0:T(8,128)(2,1)} fusion(bf16[16,16,2048]{0,1,2:T(8,128)(2,1)} %copy.27), kind=kLoop, calls=%fused_computation.79 | loop fusion | bytes 2097152
  312.8 11.3 %reshape.109 = bf16[8,2,32768]{2,1,0:T(2,128)(2,1)} reshape(bf16[2048,16,16]{2,1,0:T(8,128)(2,1)} %bitcast_bitcast_fusion) | data formatting | bytes 2097152
  324.0 5.9 %all-to-all-start.3 = ((bf16[8,2,32768]{2,1,0:T(2,128)(2,1)}), bf16[8,2,32768]{2,1,0:T(2,128)(2,1)S(1)}, u32[]{:S(2)}, u32[]{:S(2)}) async-start(bf16[8,2,32768]{2,1,0:T(2,128)(2,1)} %reshape.109), calls=%async_computation.3 | async-start | bytes 2097152 | tf_op jit(solution)/shard_map/all_to_all | solution.py:89
  330.0 3.9 %fusion.23 = f32[1,256]{1,0:T(1,128)S(1)} fusion(bf16[1024,1]{0,1:T(2,128)(2,1)S(1)} %reshape.105, bf16[256,2048]{1,0:T(8,128)(2,1)} %copy-done.9, bf16[2048,1024]{1,0:T(8,128)(2,1)} %param.18), kind=kOutput, calls=%fused_computation.41 | convolution fusion | flops 1075576832 | bytes 5245952 | tf_op jit(solution)/shard_map/dot_general | solution.py:86
  334.0 4.0 %fusion.24 = f32[1,256]{1,0:T(1,128)S(1)} fusion(bf16[1024,1]{0,1:T(2,128)(2,1)S(1)} %reshape.105, bf16[256,2048]{1,0:T(8,128)(2,1)} %copy-done.8, bf16[2048,1024]{1,0:T(8,128)(2,1)} %param.18), kind=kOutput, calls=%fused_computation.42 | convolution fusion | flops 1075576832 | bytes 5245952 | tf_op jit(solution)/shard_map/dot_general | solution.py:86
  338.7 7.6 %reshape.112 = bf16[2048,16,16]{2,1,0:T(8,128)(2,1)} reshape(bf16[8,2,32768]{2,1,0:T(2,128)(2,1)S(1)} %all-to-all-done.1) | data formatting | bytes 2097152
  346.3 9.1 %copy.26 = bf16[16,256,8,16]{1,3,2,0:T(8,128)(2,1)} copy(bf16[16,256,8,16]{3,0,1,2:T(8,128)(2,1)} %bitcast.72) | data formatting | bytes 2097152 | tf_op jit(solution)/shard_map/all_to_all | solution.py:89
  355.4 7.6 %reshape.110 = bf16[2048,16,16]{2,1,0:T(8,128)(2,1)} reshape(bf16[8,2,32768]{2,1,0:T(2,128)(2,1)S(1)} %all-to-all-done.3) | data formatting | bytes 2097152
  363.0 9.1 %copy.29 = bf16[16,256,8,16]{1,3,2,0:T(8,128)(2,1)} copy(bf16[16,256,8,16]{3,0,1,2:T(8,128)(2,1)} %bitcast.73) | data formatting | bytes 2097152 | tf_op jit(solution)/shard_map/all_to_all | solution.py:89
  (87 shorter events, 60.3 us)
Async XLA Ops:
  7.2 219.1 %copy-start = (bf16[256,2048]{1,0:T(8,128)(2,1)S(1)}, bf16[256,2048]{1,0:T(8,128)(2,1)}, u32[]{:S(2)}) copy-start(bf16[256,2048]{1,0:T(8,128)(2,1)} %param.16) | copy-start | bytes 3145732
  7.2 130.6 %all-gather.4.cloned.1.call-start = ((), (), s32[]{:S(2)}) async-start(), calls=%async_computation.4 | async-start | bytes 9437184 | tf_op jit(solution)/shard_map/all_gather | solution.py:56
  9.6 49.5 %collective-permute-start = (bf16[256,2048]{1,0:T(8,128)(2,1)S(1)}, bf16[256,2048]{1,0:T(8,128)(2,1)}, u32[]{:S(2)}, u32[]{:S(2)}) collective-permute-start(bf16[256,2048]{1,0:T(8,128)(2,1)S(1)} %bitcast.74), channel_id=1, source_target_pairs={{0,8},{8,16},{16,24},{24,0},{1,9},{9,17},{17,25},{25,1},{2,10},{10... | collective-permute-start | bytes 3145736 | tf_op jit(solution)/shard_map/ppermute | solution.py:16
  10.1 49.3 %collective-permute-start.3 = (bf16[256,2048]{1,0:T(8,128)(2,1)S(1)}, bf16[256,2048]{1,0:T(8,128)(2,1)}, u32[]{:S(2)}, u32[]{:S(2)}) collective-permute-start(bf16[256,2048]{1,0:T(8,128)(2,1)S(1)} %bitcast.78), channel_id=1, source_target_pairs={{0,8},{8,16},{16,24},{24,0},{1,9},{9,17},{17,25},{25,1},{2,10},{10... | collective-permute-start | bytes 3145736 | tf_op jit(solution)/shard_map/ppermute | solution.py:16
  12.7 53.8 %collective-permute-start.1 = (bf16[256,2048]{1,0:T(8,128)(2,1)S(1)}, bf16[256,2048]{1,0:T(8,128)(2,1)}, u32[]{:S(2)}, u32[]{:S(2)}) collective-permute-start(bf16[256,2048]{1,0:T(8,128)(2,1)S(1)} %bitcast.75), channel_id=1, source_target_pairs={{0,24},{8,0},{16,8},{24,16},{1,25},{9,1},{17,9},{25,17},{2,26},{10... | collective-permute-start | bytes 3145736 | tf_op jit(solution)/shard_map/ppermute | solution.py:21
  12.7 56.1 %collective-permute-start.4 = (bf16[256,2048]{1,0:T(8,128)(2,1)S(1)}, bf16[256,2048]{1,0:T(8,128)(2,1)}, u32[]{:S(2)}, u32[]{:S(2)}) collective-permute-start(bf16[256,2048]{1,0:T(8,128)(2,1)S(1)} %bitcast.79), channel_id=1, source_target_pairs={{0,24},{8,0},{16,8},{24,16},{1,25},{9,1},{17,9},{25,17},{2,26},{10... | collective-permute-start | bytes 3145736 | tf_op jit(solution)/shard_map/ppermute | solution.py:21
  13.4 3.8 copy-start.4
  13.5 4.1 %copy-start.1 = (bf16[1024,2048]{1,0:T(8,128)(2,1)}, bf16[1024,2048]{1,0:T(8,128)(2,1)S(1)}, u32[]{:S(2)}) copy-start(bf16[1024,2048]{1,0:T(8,128)(2,1)S(1)} %constant_dynamic-update-slice_fusion.7) | copy-start | bytes 12582916
  13.5 4.1 %copy-start.14 = (s32[1,2]{1,0:T(1,128)S(1)}, s32[1,2]{1,0:T(1,128)}, u32[]{:S(2)}) copy-start(s32[1,2]{1,0:T(1,128)} %param.13) | copy-start | bytes 28
  13.5 48.0 %copy-start.11 = (bf16[1,2048]{1,0:T(2,128)(2,1)S(1)}, bf16[1,2048]{1,0:T(2,128)(2,1)}, u32[]{:S(2)}) copy-start(bf16[1,2048]{1,0:T(2,128)(2,1)} %param.15) | copy-start | bytes 12292
  59.1 15.0 %collective-permute-start.2 = (bf16[256,2048]{1,0:T(8,128)(2,1)}, bf16[256,2048]{1,0:T(8,128)(2,1)}, u32[]{:S(2)}, u32[]{:S(2)}) collective-permute-start(bf16[256,2048]{1,0:T(8,128)(2,1)} %collective-permute-done), channel_id=1, source_target_pairs={{0,8},{8,16},{16,24},{24,0},{1,9},{9,17},{17,25},{25,1},{2,10},{10... | collective-permute-start | bytes 3145736 | tf_op jit(solution)/shard_map/ppermute | solution.py:16
  59.4 25.9 %collective-permute-start.5 = (bf16[256,2048]{1,0:T(8,128)(2,1)}, bf16[256,2048]{1,0:T(8,128)(2,1)}, u32[]{:S(2)}, u32[]{:S(2)}) collective-permute-start(bf16[256,2048]{1,0:T(8,128)(2,1)} %collective-permute-done.3), channel_id=1, source_target_pairs={{0,8},{8,16},{16,24},{24,0},{1,9},{9,17},{17,25},{25,1},{2,10},{10... | collective-permute-start | bytes 3145736 | tf_op jit(solution)/shard_map/ppermute | solution.py:16
  153.6 53.2 %all-to-all-start.2 = ((bf16[4,256,2048]{2,1,0:T(8,128)(2,1)}), bf16[4,256,2048]{2,1,0:T(8,128)(2,1)}, u32[]{:S(2)}, u32[]{:S(2)}) async-start(bf16[4,256,2048]{2,1,0:T(8,128)(2,1)} %multiply_convert_fusion), calls=%async_computation.2 | async-start | bytes 8388608 | tf_op jit(solution)/shard_map/all_to_all | solution.py:72
  158.7 3.5 copy-start.2
  176.7 35.3 %copy-start.10 = (s32[1,2,2,16,16]{4,3,2,1,0:T(8,128)S(1)}, s32[1,2,2,16,16]{4,3,2,1,0:T(8,128)}, u32[]{:S(2)}) copy-start(s32[1,2,2,16,16]{4,3,2,1,0:T(8,128)} %param.12) | copy-start | bytes 12292
  176.7 35.6 %copy-start.12 = (bf16[2048]{0:T(1024)(128)(2,1)S(1)}, bf16[2048]{0:T(1024)(128)(2,1)}, u32[]{:S(2)}) copy-start(bf16[2048]{0:T(1024)(128)(2,1)} %param.17) | copy-start | bytes 12292
  206.8 53.1 %all-to-all-start = ((bf16[4,256,2048]{2,1,0:T(8,128)(2,1)}), bf16[4,256,2048]{2,1,0:T(8,128)(2,1)}, u32[]{:S(2)}, u32[]{:S(2)}) async-start(bf16[4,256,2048]{2,1,0:T(8,128)(2,1)} %multiply_convert_fusion.1), calls=%async_computation | async-start | bytes 8388608 | tf_op jit(solution)/shard_map/all_to_all | solution.py:72
  221.6 6.7 %copy-start.6 = (f32[512,2048]{1,0:T(8,128)}, f32[512,2048]{1,0:T(8,128)S(1)}, u32[]{:S(2)}) copy-start(f32[512,2048]{1,0:T(8,128)S(1)} %bitcast_add_fusion) | copy-start | bytes 12582916
  259.9 3.4 copy-start.7
  265.3 8.8 %copy-start.9 = (bf16[256,2048]{1,0:T(8,128)(2,1)}, bf16[256,2048]{1,0:T(8,128)(2,1)S(1)}, u32[]{:S(2)}) copy-start(bf16[256,2048]{1,0:T(8,128)(2,1)S(1)} %get-tuple-element.14) | copy-start | bytes 3145732
  265.3 31.1 %copy-start.8 = (bf16[256,2048]{1,0:T(8,128)(2,1)}, bf16[256,2048]{1,0:T(8,128)(2,1)S(1)}, u32[]{:S(2)}) copy-start(bf16[256,2048]{1,0:T(8,128)(2,1)S(1)} %get-tuple-element.15) | copy-start | bytes 3145732
  292.9 31.1 %all-to-all-start.1 = ((bf16[8,2,32768]{2,1,0:T(2,128)(2,1)}), bf16[8,2,32768]{2,1,0:T(2,128)(2,1)S(1)}, u32[]{:S(2)}, u32[]{:S(2)}) async-start(bf16[8,2,32768]{2,1,0:T(2,128)(2,1)} %reshape.111), calls=%async_computation.1 | async-start | bytes 2097152 | tf_op jit(solution)/shard_map/all_to_all | solution.py:89
  312.8 17.2 %copy-start.13 = (bf16[1024]{0:T(1024)(128)(2,1)S(1)}, bf16[1024]{0:T(1024)(128)(2,1)}, u32[]{:S(2)}) copy-start(bf16[1024]{0:T(1024)(128)(2,1)} %param.19) | copy-start | bytes 6148
  324.0 31.4 %all-to-all-start.3 = ((bf16[8,2,32768]{2,1,0:T(2,128)(2,1)}), bf16[8,2,32768]{2,1,0:T(2,128)(2,1)S(1)}, u32[]{:S(2)}, u32[]{:S(2)}) async-start(bf16[8,2,32768]{2,1,0:T(2,128)(2,1)} %reshape.109), calls=%async_computation.3 | async-start | bytes 2097152 | tf_op jit(solution)/shard_map/all_to_all | solution.py:89
  (2 other events, 3.9 us)
Sparse Core Ops, SparseCore 0:
  10.1 127.6 all-gather.3
